TPU v7x, 32 devices: a whole 2x2x4 slice. The times are simulated.
32 devices in a mesh: grp: 2 (over x), gx: 8 (over z, y), gy: 2 (over core).
Axes of the slice: x: 2, y: 2, z: 4, core: 2. Of those that a mesh axis runs over, the one named last changes fastest.
Arguments:
- spectrum: float32 [16, 96, 1152], P('gx', 'gy', 'grp'), may hold values from 0 to 2
- wet_mask: int32 [16, 96], P('gx', 'gy'), may hold values 0 or 1
- ocean_source: int32 [16, 96], P('gx', 'gy'), may hold values from 0 to 95
- ocean_u: float32 [16, 96, 40], P('gx', 'gy', 'grp'), may hold values from -2 to 2
- ocean_v: float32 [16, 96, 40], P('gx', 'gy', 'grp'), may hold values from -2 to 2
- current_weights: float32 [40, 32], replicated, may hold values from 0.005 to 0.04
- drift_weights: float32 [40, 32], replicated, may hold values from 0.005 to 0.05
- inter_left: bfloat16 [1152, 512], P('grp'), may hold values from -0.25 to 0.25
- inter_right: bfloat16 [1152, 512], P('grp'), may hold values from -0.25 to 0.25
- inter_out: bfloat16 [512, 1152], P(None, 'grp'), may hold values from -0.25 to 0.25
- mixing: float32 [40, 40], P(None, 'grp'), may hold values from -0.47434166 to 0.47434166
Outputs:
- spectrum_out: float32 [16, 96, 1152], P('gx', 'gy', 'grp')
- ocean_u_out: float32 [16, 96, 40], P('gx', 'gy', 'grp')
- ocean_v_out: float32 [16, 96, 40], P('gx', 'gy', 'grp')
- drift_u: float32 [16, 96, 40], P('gx', 'gy', 'grp')
- drift_v: float32 [16, 96, 40], P('gx', 'gy', 'grp')
Inputs may be any that keep to these rules, and one draw needn't show every extreme that they name: `wet_mask`: 1 marks a sea column, 0 a land column. `ocean_source`: each entry numbers a column of the same tile of 2 x 48 columns as (x mod 2) * 48 + (y mod 48).
All inputs are finite; a program needn't handle non-finite values. No bound on the sum of `wet_mask` on one device may be relied on, other than what follows from the above.
Results may differ from a plain program's by a relative error of at most 0.00077.
Values sent between devices are 32-bit elements; how exact they have to be, the bound alone decides.
A program may use at most 64 MiB of HBM per device.

v0:
```python
import jax
import jax.numpy as jnp
from jax import lax
from jax.sharding import PartitionSpec as P

NF = 32
ND = 36
NLEV = 40
WAVE_SECTIONS = 3
OCEAN_SECTIONS = 2
NFL = 16
highest = lax.Precision.HIGHEST
inter_step = 0.1
ocean_step = 0.4
coriolis = 0.5
viscosity = 0.1


def extended(array, sides, width):
    for axis, dim in sides:
        size, length = (lax.axis_size(axis), array.shape[dim])
        up = [(i, (i + 1) % size) for i in range(size - 1)]
        down = [(j, i) for i, j in up]
        last = lax.slice_in_dim(array, length - width, length, axis=dim)
        leading = lax.slice_in_dim(array, 0, width, axis=dim)
        before = lax.ppermute(last, axis, up)
        after = lax.ppermute(leading, axis, down)
        array = jnp.concatenate([before, array, after], axis=dim)
    return array


def bin_tables(band_index, bin_count):
    position = jnp.arange(bin_count)
    direction = (position // NFL).astype(jnp.float32)
    frequency = (band_index * NFL + position % NFL).astype(jnp.float32)
    angle_value = 2.0 * jnp.pi * direction / ND
    group_speed = 0.2 + 0.4 * (NF - 1 - frequency) / (NF - 1)
    turning = 0.5 * (frequency + 1.0) / NF
    return (jnp.cos(angle_value), jnp.sin(angle_value), group_speed, turning)


def beam_sweep(padded, velocity, which_axis):
    extent = velocity.shape[which_axis]

    def take_part(offset):
        return lax.slice_in_dim(padded, offset, offset + extent, axis=which_axis)

    centre = take_part(2)
    upwind_one = jnp.where(velocity >= 0.0, take_part(1), take_part(3))
    beyond = jnp.where(velocity >= 0.0, take_part(0), take_part(4))
    magnitude = jnp.abs(velocity)
    return (
        centre
        - 0.5 * magnitude * (3.0 * centre - 4.0 * upwind_one + beyond)
        + 0.5 * magnitude * magnitude * (centre - 2.0 * upwind_one + beyond)
    )


def body(
    spectrum,
    wet_mask,
    ocean_source,
    ocean_u,
    ocean_v,
    current_weights,
    drift_weights,
    inter_left,
    inter_right,
    inter_out,
    mixing,
):
    band_index = lax.axis_index("grp")
    tile_x = spectrum.shape[0]
    tile_y = spectrum.shape[1]
    bin_count = spectrum.shape[2]
    levels_own = ocean_u.shape[2]
    cosine, sine_value, group_speed, turning = bin_tables(band_index, bin_count)
    wet_factor = wet_mask.astype(jnp.float32)[:, :, None]
    flat_source = ocean_source.reshape(-1)
    whole_u, whole_v = (
        lax.all_gather(ocean_u, "grp", axis=2, tiled=True),
        lax.all_gather(ocean_v, "grp", axis=2, tiled=True),
    )
    weights_band = lax.dynamic_slice_in_dim(current_weights, band_index * NFL, NFL, 1)
    picked_u = jnp.take(whole_u.reshape(tile_x * tile_y, NLEV), flat_source, axis=0)
    picked_v = jnp.take(whole_v.reshape(tile_x * tile_y, NLEV), flat_source, axis=0)
    flow_x = jnp.dot(picked_u, weights_band, precision=highest, preferred_element_type=jnp.float32)
    flow_y = jnp.dot(picked_v, weights_band, precision=highest, preferred_element_type=jnp.float32)
    flow_x = flow_x.reshape(tile_x, tile_y, NFL)
    flow_y = flow_y.reshape(tile_x, tile_y, NFL)
    flow_x_bins = jnp.tile(flow_x, (1, 1, ND))
    flow_y_bins = jnp.tile(flow_y, (1, 1, ND))
    speed_y = group_speed * sine_value + flow_y_bins
    turn_rate = turning * (sine_value * flow_x_bins - cosine * flow_y_bins)
    current_pad = extended(jnp.concatenate([flow_x, flow_y], axis=2), (("gx", 0), ("gy", 1)), 2)
    speed_x_wide = group_speed * cosine + jnp.tile(current_pad[2 : tile_x + 2, :, :NFL], (1, 1, ND))
    spectrum_now = wet_factor * spectrum
    for repeat in range(WAVE_SECTIONS):
        padded = extended(spectrum_now, (("gx", 0), ("gy", 1)), 2)
        shifted = beam_sweep(padded, speed_x_wide, 0)
        shifted = beam_sweep(shifted, speed_y, 1)
        behind = jnp.roll(shifted, NFL, axis=2)
        ahead_dir = jnp.roll(shifted, -NFL, axis=2)
        upwind = jnp.where(turn_rate >= 0.0, behind, ahead_dir)
        turned = shifted - jnp.abs(turn_rate) * (shifted - upwind)
        flat_bins = spectrum_now.reshape(-1, bin_count).astype(jnp.bfloat16)
        product = jnp.dot(flat_bins, inter_left, preferred_element_type=jnp.float32) * jnp.dot(
            flat_bins, inter_right, preferred_element_type=jnp.float32
        )
        source = inter_step * jnp.dot(
            product.astype(jnp.bfloat16), inter_out, preferred_element_type=jnp.float32
        )
        spectrum_now = wet_factor * (turned + source.reshape(spectrum_now.shape))
    profile = jnp.tile(lax.dynamic_slice_in_dim(drift_weights, band_index * NFL, NFL, 1), (1, ND))
    final_flat = spectrum_now.reshape(-1, bin_count)
    contract = (((1,), (1,)), ((), ()))
    part_x = lax.dot_general(
        final_flat,
        profile * cosine,
        contract,
        precision=highest,
        preferred_element_type=jnp.float32,
    )
    part_y = lax.dot_general(
        final_flat,
        profile * sine_value,
        contract,
        precision=highest,
        preferred_element_type=jnp.float32,
    )
    drift_x, drift_y = (
        lax.psum_scatter(part_x, "grp", scatter_dimension=1, tiled=True),
        lax.psum_scatter(part_y, "grp", scatter_dimension=1, tiled=True),
    )
    drift_x = drift_x.reshape(tile_x, tile_y, levels_own)
    drift_y = drift_y.reshape(tile_x, tile_y, levels_own)
    velocity_u = ocean_u
    velocity_v = ocean_v
    for repeat in range(OCEAN_SECTIONS):
        stacked = jnp.concatenate([velocity_u, velocity_v], axis=2)
        padded = extended(stacked, (("gx", 0), ("gy", 1)), 1)
        laplace_both = (
            padded[2:, 1:-1]
            + padded[:-2, 1:-1]
            + padded[1:-1, 2:]
            + padded[1:-1, :-2]
            - 4.0 * stacked
        )
        laplace_u = laplace_both[:, :, :levels_own]
        laplace_v = laplace_both[:, :, levels_own:]
        first_u = velocity_u + ocean_step * (
            coriolis * (velocity_v + drift_y) + viscosity * laplace_u
        )
        first_v = velocity_v + ocean_step * (
            -coriolis * (velocity_u + drift_x) + viscosity * laplace_v
        )
        whole_u, whole_v = (
            lax.all_gather(first_u, "grp", axis=2, tiled=True),
            lax.all_gather(first_v, "grp", axis=2, tiled=True),
        )
        velocity_u = wet_factor * (
            first_u + jnp.einsum("abk,kl->abl", whole_u, mixing, precision=highest)
        )
        velocity_v = wet_factor * (
            first_v + jnp.einsum("abk,kl->abl", whole_v, mixing, precision=highest)
        )
    return (spectrum_now, velocity_u, velocity_v, drift_x, drift_y)


def solution(mesh):
    in_specs = (
        P("gx", "gy", "grp"),
        P("gx", "gy"),
        P("gx", "gy"),
        P("gx", "gy", "grp"),
        P("gx", "gy", "grp"),
        P(),
        P(),
        P("grp", None),
        P("grp", None),
        P(None, "grp"),
        P(None, "grp"),
    )
    out_specs = (
        P("gx", "gy", "grp"),
        P("gx", "gy", "grp"),
        P("gx", "gy", "grp"),
        P("gx", "gy", "grp"),
        P("gx", "gy", "grp"),
    )
    return jax.shard_map(body, mesh=mesh, in_specs=in_specs, out_specs=out_specs, check_vma=False)
```

profile of v0, /device:TPU:24, one launch (start us, length us, event | category | flops | bytes accessed | tf_op | source)
XLA Modules:
  0.0 159.7 jit_solution(4556036495489061007)
XLA Ops:
  1.5 4.5 %all_gather.18 = f32[2,48,40]{1,0,2:T(2,128)S(1)} all-gather(f32[2,48,20]{1,0,2:T(2,128)S(1)} %copy-done.17), channel_id=1, replica_groups=mesh['grp'=2,'gx'=8,'gy'=2] {'grp'}, dimensions={2}, use_global_device_ids=true | all-gather | bytes 23040 | tf_op jit(solution)/shard_map/all_gather | solution.py:81
  7.8 4.4 %all_gather.19 = f32[2,48,40]{1,0,2:T(2,128)S(1)} all-gather(f32[2,48,20]{1,0,2:T(2,128)S(1)} %copy-done.18), channel_id=1, replica_groups=mesh['grp'=2,'gx'=8,'gy'=2] {'grp'}, dimensions={2}, use_global_device_ids=true | all-gather | bytes 23040 | tf_op jit(solution)/shard_map/all_gather | solution.py:82
  13.4 3.4 %collective-permute-start.4 = (f32[2,48,32]{1,0,2:T(2,128)S(1)}, f32[2,48,32]{1,0,2:T(2,128)}, u32[]{:S(2)}, u32[]{:S(2)}) collective-permute-start(f32[2,48,32]{1,0,2:T(2,128)S(1)} %constant_dynamic-update-slice_fusion), channel_id=1, source_target_pairs={{0,2},{2,4},{4,6},{6,8},{8,10},{10,12},{12,14},{1,3},{3,5},{5,7},{... | collective-permute-start | bytes 36872 | tf_op jit(solution)/shard_map/ppermute | solution.py:26
  16.8 3.3 %collective-permute-start.5 = (f32[2,48,32]{1,0,2:T(2,128)S(1)}, f32[2,48,32]{1,0,2:T(2,128)}, u32[]{:S(2)}, u32[]{:S(2)}) collective-permute-start(f32[2,48,32]{1,0,2:T(2,128)S(1)} %constant_dynamic-update-slice_fusion), channel_id=1, source_target_pairs={{2,0},{4,2},{6,4},{8,6},{10,8},{12,10},{14,12},{3,1},{5,3},{7,5},{... | collective-permute-start | bytes 36872 | tf_op jit(solution)/shard_map/ppermute | solution.py:27
  20.7 3.2 %collective-permute-start = (f32[2,48,576]{2,1,0:T(8,128)S(1)}, f32[2,48,576]{2,1,0:T(8,128)S(1)}, u32[]{:S(2)}, u32[]{:S(2)}) collective-permute-start(f32[2,48,576]{2,1,0:T(8,128)S(1)} %get-tuple-element.49), channel_id=1, source_target_pairs={{0,2},{2,4},{4,6},{6,8},{8,10},{10,12},{12,14},{1,3},{3,5},{5,7},{... | collective-permute-start | bytes 663560 | tf_op jit(solution)/shard_map/ppermute | solution.py:26
  24.6 3.6 %collective-permute-start.16 = (f32[1,48,40]{1,2,0:T(8,128)}, f32[1,48,40]{1,2,0:T(8,128)}, u32[]{:S(2)}, u32[]{:S(2)}) collective-permute-start(f32[1,48,40]{1,2,0:T(8,128)} %get-tuple-element.81), channel_id=1, source_target_pairs={{2,0},{4,2},{6,4},{8,6},{10,8},{12,10},{14,12},{3,1},{5,3},{7,5},{... | collective-permute-start | bytes 23048 | tf_op jit(solution)/shard_map/ppermute | solution.py:27
  28.2 2.8 %collective-permute-start.17 = (f32[1,48,40]{1,2,0:T(8,128)}, f32[1,48,40]{1,2,0:T(8,128)}, u32[]{:S(2)}, u32[]{:S(2)}) collective-permute-start(f32[1,48,40]{1,2,0:T(8,128)} %get-tuple-element.80), channel_id=1, source_target_pairs={{0,2},{2,4},{4,6},{6,8},{8,10},{10,12},{12,14},{1,3},{3,5},{5,7},{... | collective-permute-start | bytes 23048 | tf_op jit(solution)/shard_map/ppermute | solution.py:26
  32.7 1.2 convolution_multiply_fusion.2
  33.9 0.9 broadcast_multiply_fusion
  37.1 1.3 collective-permute-start.18
  38.4 4.3 %collective-permute-start.19 = (f32[4,1,40]{1,2,0:T(8,128)}, f32[4,1,40]{1,2,0:T(8,128)}, u32[]{:S(2)}, u32[]{:S(2)}) collective-permute-start(f32[4,1,40]{1,2,0:T(8,128)} %get-tuple-element.77), channel_id=1, source_target_pairs={{0,1},{2,3},{4,5},{6,7},{8,9},{10,11},{12,13},{14,15},{16,17},{18,... | collective-permute-start | bytes 1928 | tf_op jit(solution)/shard_map/ppermute | solution.py:26
  42.7 0.9 copy.297
  45.5 4.0 %collective-permute-start.1 = (f32[2,48,576]{2,1,0:T(8,128)S(1)}, f32[2,48,576]{2,1,0:T(8,128)S(1)}, u32[]{:S(2)}, u32[]{:S(2)}) collective-permute-start(f32[2,48,576]{2,1,0:T(8,128)S(1)} %get-tuple-element.49), channel_id=1, source_target_pairs={{2,0},{4,2},{6,4},{8,6},{10,8},{12,10},{14,12},{3,1},{5,3},{7,5},{... | collective-permute-start | bytes 663560 | tf_op jit(solution)/shard_map/ppermute | solution.py:27
  49.5 0.9 fusion.41
  51.4 1.3 collective-permute-start.6
  52.7 1.3 collective-permute-start.7
  54.9 3.6 %collective-permute-start.2 = (f32[6,2,576]{2,1,0:T(2,128)}, f32[6,2,576]{2,1,0:T(2,128)}, u32[]{:S(2)}, u32[]{:S(2)}) collective-permute-start(f32[6,2,576]{2,1,0:T(2,128)} %get-tuple-element.54), channel_id=1, source_target_pairs={{0,1},{2,3},{4,5},{6,7},{8,9},{10,11},{12,13},{14,15},{16,17},{18,... | collective-permute-start | bytes 82952 | tf_op jit(solution)/shard_map/ppermute | solution.py:26
  58.5 1.3 collective-permute-start.3
  61.0 0.9 collective-permute-done.3
  61.9 1.2 pad_maximum_fusion
  65.3 1.9 %collective-permute-start.8 = (f32[2,48,576]{2,1,0:T(8,128)S(1)}, f32[2,48,576]{2,1,0:T(8,128)S(1)}, u32[]{:S(2)}, u32[]{:S(2)}) collective-permute-start(f32[2,48,576]{2,1,0:T(8,128)S(1)} %get-tuple-element.46), channel_id=1, source_target_pairs={{0,2},{2,4},{4,6},{6,8},{8,10},{10,12},{12,14},{1,3},{3,5},{5,7},{... | collective-permute-start | bytes 663560 | tf_op jit(solution)/shard_map/ppermute | solution.py:26
  67.2 4.8 %collective-permute-start.9 = (f32[2,48,576]{2,1,0:T(8,128)S(1)}, f32[2,48,576]{2,1,0:T(8,128)S(1)}, u32[]{:S(2)}, u32[]{:S(2)}) collective-permute-start(f32[2,48,576]{2,1,0:T(8,128)S(1)} %get-tuple-element.46), channel_id=1, source_target_pairs={{2,0},{4,2},{6,4},{8,6},{10,8},{12,10},{14,12},{3,1},{5,3},{7,5},{... | collective-permute-start | bytes 663560 | tf_op jit(solution)/shard_map/ppermute | solution.py:27
  72.0 0.9 fusion.119
  73.0 3.9 %collective-permute-done.8 = f32[2,48,576]{2,1,0:T(8,128)S(1)} collective-permute-done((f32[2,48,576]{2,1,0:T(8,128)S(1)}, f32[2,48,576]{2,1,0:T(8,128)S(1)}, u32[]{:S(2)}, u32[]{:S(2)}) %collective-permute-start.8) | collective-permute-done | bytes 221216 | tf_op jit(solution)/shard_map/ppermute | solution.py:26
  76.8 5.2 %collective-permute-done.9 = f32[2,48,576]{2,1,0:T(8,128)S(1)} collective-permute-done((f32[2,48,576]{2,1,0:T(8,128)S(1)}, f32[2,48,576]{2,1,0:T(8,128)S(1)}, u32[]{:S(2)}, u32[]{:S(2)}) %collective-permute-start.9) | collective-permute-done | bytes 221216 | tf_op jit(solution)/shard_map/ppermute | solution.py:27
  82.7 2.6 %collective-permute-start.10 = (f32[6,2,576]{2,1,0:T(2,128)}, f32[6,2,576]{2,1,0:T(2,128)}, u32[]{:S(2)}, u32[]{:S(2)}) collective-permute-start(f32[6,2,576]{2,1,0:T(2,128)} %get-tuple-element.52), channel_id=1, source_target_pairs={{0,1},{2,3},{4,5},{6,7},{8,9},{10,11},{12,13},{14,15},{16,17},{18,... | collective-permute-start | bytes 82952 | tf_op jit(solution)/shard_map/ppermute | solution.py:26
  85.3 1.3 collective-permute-start.11
  86.6 2.1 %convolution_multiply_fusion.1 = f32[96,576]{1,0:T(8,128)} fusion(bf16[512,576]{0,1:T(8,128)(2,1)S(1)} %copy-done, f32[96,512]{1,0:T(8,128)} %fusion.119, bf16[96,576]{1,0:T(8,128)(2,1)S(1)} %bitcast.65, bf16[576,512]{1,0:T(8,128)(2,1)S(1)} %copy-done.2), kind=kOutput, calls=%fused_computation.3 | convolution fusion | flops 113399808 | bytes 1708032 | tf_op jit(solution)/shard_map/dot_general | solution.py:110
  88.7 1.1 pad_maximum_fusion.1
  91.3 1.9 %collective-permute-start.12 = (f32[2,48,576]{2,1,0:T(8,128)S(1)}, f32[2,48,576]{2,1,0:T(8,128)S(1)}, u32[]{:S(2)}, u32[]{:S(2)}) collective-permute-start(f32[2,48,576]{2,1,0:T(8,128)S(1)} %get-tuple-element.44), channel_id=1, source_target_pairs={{0,2},{2,4},{4,6},{6,8},{8,10},{10,12},{12,14},{1,3},{3,5},{5,7},{... | collective-permute-start | bytes 663560 | tf_op jit(solution)/shard_map/ppermute | solution.py:26
  93.2 4.8 %collective-permute-start.13 = (f32[2,48,576]{2,1,0:T(8,128)S(1)}, f32[2,48,576]{2,1,0:T(8,128)S(1)}, u32[]{:S(2)}, u32[]{:S(2)}) collective-permute-start(f32[2,48,576]{2,1,0:T(8,128)S(1)} %get-tuple-element.44), channel_id=1, source_target_pairs={{2,0},{4,2},{6,4},{8,6},{10,8},{12,10},{14,12},{3,1},{5,3},{7,5},{... | collective-permute-start | bytes 663560 | tf_op jit(solution)/shard_map/ppermute | solution.py:27
  98.1 0.9 fusion.120
  99.0 3.3 %collective-permute-done.12 = f32[2,48,576]{2,1,0:T(8,128)S(1)} collective-permute-done((f32[2,48,576]{2,1,0:T(8,128)S(1)}, f32[2,48,576]{2,1,0:T(8,128)S(1)}, u32[]{:S(2)}, u32[]{:S(2)}) %collective-permute-start.12) | collective-permute-done | bytes 221216 | tf_op jit(solution)/shard_map/ppermute | solution.py:26
  102.3 5.8 %collective-permute-done.13 = f32[2,48,576]{2,1,0:T(8,128)S(1)} collective-permute-done((f32[2,48,576]{2,1,0:T(8,128)S(1)}, f32[2,48,576]{2,1,0:T(8,128)S(1)}, u32[]{:S(2)}, u32[]{:S(2)}) %collective-permute-start.13) | collective-permute-done | bytes 221216 | tf_op jit(solution)/shard_map/ppermute | solution.py:27
  108.8 2.0 %collective-permute-start.14 = (f32[6,2,576]{2,1,0:T(2,128)}, f32[6,2,576]{2,1,0:T(2,128)S(1)}, u32[]{:S(2)}, u32[]{:S(2)}) collective-permute-start(f32[6,2,576]{2,1,0:T(2,128)} %get-tuple-element.50), channel_id=1, source_target_pairs={{0,1},{2,3},{4,5},{6,7},{8,9},{10,11},{12,13},{14,15},{16,17},{18,... | collective-permute-start | bytes 82952 | tf_op jit(solution)/shard_map/ppermute | solution.py:26
  110.9 1.4 collective-permute-start.15
  112.3 1.4 convolution_multiply_fusion
  117.1 8.5 %all-reduce.2 = (f32[96,40]{0,1:T(8,128)S(1)}, f32[96,40]{0,1:T(8,128)S(1)}) all-reduce(f32[96,40]{0,1:T(8,128)S(1)} %fusion.121, f32[96,40]{0,1:T(8,128)S(1)} %fusion.122), channel_id=2, replica_groups=mesh['grp'=2,'gx'=8,'gy'=2] {'grp'}, use_global_device_ids=true, to_apply=%region_0.2.clone | all-reduce | flops 7680 | bytes 61440
  125.9 4.5 %all_gather.20 = f32[2,48,40]{1,0,2:T(2,128)S(1)} all-gather(f32[2,48,20]{1,0,2:T(2,128)S(1)} %copy.304), channel_id=1, replica_groups=mesh['grp'=2,'gx'=8,'gy'=2] {'grp'}, dimensions={2}, use_global_device_ids=true | all-gather | bytes 23040 | tf_op jit(solution)/shard_map/all_gather | solution.py:158
  130.3 4.5 %all_gather.21 = f32[2,48,40]{1,0,2:T(2,128)S(1)} all-gather(f32[2,48,20]{1,0,2:T(2,128)S(1)} %copy.309), channel_id=1, replica_groups=mesh['grp'=2,'gx'=8,'gy'=2] {'grp'}, dimensions={2}, use_global_device_ids=true | all-gather | bytes 23040 | tf_op jit(solution)/shard_map/all_gather | solution.py:159
  135.2 1.9 %collective-permute-start.20 = (f32[1,48,40]{1,2,0:T(8,128)S(1)}, f32[1,48,40]{1,2,0:T(8,128)S(1)}, u32[]{:S(2)}, u32[]{:S(2)}) collective-permute-start(f32[1,48,40]{1,2,0:T(8,128)S(1)} %get-tuple-element.79), channel_id=1, source_target_pairs={{2,0},{4,2},{6,4},{8,6},{10,8},{12,10},{14,12},{3,1},{5,3},{7,5},{... | collective-permute-start | bytes 23048 | tf_op jit(solution)/shard_map/ppermute | solution.py:27
  137.1 3.9 %collective-permute-start.21 = (f32[1,48,40]{1,2,0:T(8,128)S(1)}, f32[1,48,40]{1,2,0:T(8,128)S(1)}, u32[]{:S(2)}, u32[]{:S(2)}) collective-permute-start(f32[1,48,40]{1,2,0:T(8,128)S(1)} %get-tuple-element.78), channel_id=1, source_target_pairs={{0,2},{2,4},{4,6},{6,8},{8,10},{10,12},{12,14},{1,3},{3,5},{5,7},{... | collective-permute-start | bytes 23048 | tf_op jit(solution)/shard_map/ppermute | solution.py:26
  141.0 2.6 %collective-permute-done.21 = f32[1,48,40]{1,2,0:T(8,128)S(1)} collective-permute-done((f32[1,48,40]{1,2,0:T(8,128)S(1)}, f32[1,48,40]{1,2,0:T(8,128)S(1)}, u32[]{:S(2)}, u32[]{:S(2)}) %collective-permute-start.21) | collective-permute-done | bytes 7712 | tf_op jit(solution)/shard_map/ppermute | solution.py:26
  143.8 1.3 collective-permute-start.22
  145.1 3.0 %collective-permute-start.23 = (f32[4,1,40]{1,2,0:T(8,128)S(1)}, f32[4,1,40]{1,2,0:T(8,128)S(1)}, u32[]{:S(2)}, u32[]{:S(2)}) collective-permute-start(f32[4,1,40]{1,2,0:T(8,128)S(1)} %get-tuple-element.73), channel_id=1, source_target_pairs={{0,1},{2,3},{4,5},{6,7},{8,9},{10,11},{12,13},{14,15},{16,17},{18,... | collective-permute-start | bytes 1928 | tf_op jit(solution)/shard_map/ppermute | solution.py:26
  148.1 0.9 collective-permute-done.23
  149.2 4.5 %all_gather.23 = f32[2,48,40]{1,0,2:T(2,128)S(1)} all-gather(f32[2,48,20]{1,0,2:T(2,128)S(1)} %copy.315), channel_id=1, replica_groups=mesh['grp'=2,'gx'=8,'gy'=2] {'grp'}, dimensions={2}, use_global_device_ids=true | all-gather | bytes 23040 | tf_op jit(solution)/shard_map/all_gather | solution.py:159
  154.4 4.5 %all_gather.22 = f32[2,48,40]{1,0,2:T(2,128)S(1)} all-gather(f32[2,48,20]{1,0,2:T(2,128)S(1)} %copy.312), channel_id=1, replica_groups=mesh['grp'=2,'gx'=8,'gy'=2] {'grp'}, dimensions={2}, use_global_device_ids=true | all-gather | bytes 23040 | tf_op jit(solution)/shard_map/all_gather | solution.py:158
  (159 shorter events, 23.8 us)
Async XLA Ops:
  0.6 32.0 %copy-start = (bf16[512,576]{0,1:T(8,128)(2,1)S(1)}, bf16[512,576]{0,1:T(8,128)(2,1)}, u32[]{:S(2)}) copy-start(bf16[512,576]{0,1:T(8,128)(2,1)} %param.22) | copy-start | bytes 1769476
  0.7 0.8 copy-start.17
  7.1 0.8 copy-start.18
  12.4 7.8 %copy-start.28 = (s32[2,48]{1,0:T(2,128)S(1)}, s32[2,48]{1,0:T(2,128)}, u32[]{:S(2)}) copy-start(s32[2,48]{1,0:T(2,128)} %param.14) | copy-start | bytes 1156
  12.4 7.8 %copy-start.13 = (f32[2,48,576]{2,1,0:T(8,128)S(1)}, f32[2,48,576]{2,1,0:T(8,128)}, u32[]{:S(2)}) copy-start(f32[2,48,576]{2,1,0:T(8,128)} %param.13) | copy-start | bytes 663556
  13.0 19.4 %copy-start.1 = (bf16[576,512]{1,0:T(8,128)(2,1)S(1)}, bf16[576,512]{1,0:T(8,128)(2,1)}, u32[]{:S(2)}) copy-start(bf16[576,512]{1,0:T(8,128)(2,1)} %param.20) | copy-start | bytes 1769476
  13.4 37.1 %collective-permute-start.4 = (f32[2,48,32]{1,0,2:T(2,128)S(1)}, f32[2,48,32]{1,0,2:T(2,128)}, u32[]{:S(2)}, u32[]{:S(2)}) collective-permute-start(f32[2,48,32]{1,0,2:T(2,128)S(1)} %constant_dynamic-update-slice_fusion), channel_id=1, source_target_pairs={{0,2},{2,4},{4,6},{6,8},{8,10},{10,12},{12,14},{1,3},{3,5},{5,7},{... | collective-permute-start | bytes 36872 | tf_op jit(solution)/shard_map/ppermute | solution.py:26
  16.8 33.7 %collective-permute-start.5 = (f32[2,48,32]{1,0,2:T(2,128)S(1)}, f32[2,48,32]{1,0,2:T(2,128)}, u32[]{:S(2)}, u32[]{:S(2)}) collective-permute-start(f32[2,48,32]{1,0,2:T(2,128)S(1)} %constant_dynamic-update-slice_fusion), channel_id=1, source_target_pairs={{2,0},{4,2},{6,4},{8,6},{10,8},{12,10},{14,12},{3,1},{5,3},{7,5},{... | collective-permute-start | bytes 36872 | tf_op jit(solution)/shard_map/ppermute | solution.py:27
  20.2 12.2 %copy-start.27 = (f32[40,32]{0,1:T(8,128)S(1)}, f32[40,32]{0,1:T(8,128)}, u32[]{:S(2)}) copy-start(f32[40,32]{0,1:T(8,128)} %param.19) | copy-start | bytes 15364
  20.7 12.0 %copy-start.2 = (bf16[576,512]{1,0:T(8,128)(2,1)S(1)}, bf16[576,512]{1,0:T(8,128)(2,1)}, u32[]{:S(2)}) copy-start(bf16[576,512]{1,0:T(8,128)(2,1)} %param.21) | copy-start | bytes 1769476
  20.7 33.3 %collective-permute-start = (f32[2,48,576]{2,1,0:T(8,128)S(1)}, f32[2,48,576]{2,1,0:T(8,128)S(1)}, u32[]{:S(2)}, u32[]{:S(2)}) collective-permute-start(f32[2,48,576]{2,1,0:T(8,128)S(1)} %get-tuple-element.49), channel_id=1, source_target_pairs={{0,2},{2,4},{4,6},{6,8},{8,10},{10,12},{12,14},{1,3},{3,5},{5,7},{... | collective-permute-start | bytes 663560 | tf_op jit(solution)/shard_map/ppermute | solution.py:26
  24.6 11.1 %collective-permute-start.16 = (f32[1,48,40]{1,2,0:T(8,128)}, f32[1,48,40]{1,2,0:T(8,128)}, u32[]{:S(2)}, u32[]{:S(2)}) collective-permute-start(f32[1,48,40]{1,2,0:T(8,128)} %get-tuple-element.81), channel_id=1, source_target_pairs={{2,0},{4,2},{6,4},{8,6},{10,8},{12,10},{14,12},{3,1},{5,3},{7,5},{... | collective-permute-start | bytes 23048 | tf_op jit(solution)/shard_map/ppermute | solution.py:27
  28.2 7.4 %collective-permute-start.17 = (f32[1,48,40]{1,2,0:T(8,128)}, f32[1,48,40]{1,2,0:T(8,128)}, u32[]{:S(2)}, u32[]{:S(2)}) collective-permute-start(f32[1,48,40]{1,2,0:T(8,128)} %get-tuple-element.80), channel_id=1, source_target_pairs={{0,2},{2,4},{4,6},{6,8},{8,10},{10,12},{12,14},{1,3},{3,5},{5,7},{... | collective-permute-start | bytes 23048 | tf_op jit(solution)/shard_map/ppermute | solution.py:26
  37.1 8.4 %collective-permute-start.18 = (f32[4,1,40]{1,2,0:T(8,128)}, f32[4,1,40]{1,2,0:T(8,128)}, u32[]{:S(2)}, u32[]{:S(2)}) collective-permute-start(f32[4,1,40]{1,2,0:T(8,128)} %get-tuple-element.76), channel_id=1, source_target_pairs={{1,0},{3,2},{5,4},{7,6},{9,8},{11,10},{13,12},{15,14},{17,16},{19,... | collective-permute-start | bytes 1928 | tf_op jit(solution)/shard_map/ppermute | solution.py:27
  38.4 11.1 %collective-permute-start.19 = (f32[4,1,40]{1,2,0:T(8,128)}, f32[4,1,40]{1,2,0:T(8,128)}, u32[]{:S(2)}, u32[]{:S(2)}) collective-permute-start(f32[4,1,40]{1,2,0:T(8,128)} %get-tuple-element.77), channel_id=1, source_target_pairs={{0,1},{2,3},{4,5},{6,7},{8,9},{10,11},{12,13},{14,15},{16,17},{18,... | collective-permute-start | bytes 1928 | tf_op jit(solution)/shard_map/ppermute | solution.py:26
  45.5 8.5 %collective-permute-start.1 = (f32[2,48,576]{2,1,0:T(8,128)S(1)}, f32[2,48,576]{2,1,0:T(8,128)S(1)}, u32[]{:S(2)}, u32[]{:S(2)}) collective-permute-start(f32[2,48,576]{2,1,0:T(8,128)S(1)} %get-tuple-element.49), channel_id=1, source_target_pairs={{2,0},{4,2},{6,4},{8,6},{10,8},{12,10},{14,12},{3,1},{5,3},{7,5},{... | collective-permute-start | bytes 663560 | tf_op jit(solution)/shard_map/ppermute | solution.py:27
  51.4 8.3 %collective-permute-start.6 = (f32[6,2,32]{1,0,2:T(8,128)S(1)}, f32[6,2,32]{1,0,2:T(8,128)S(1)}, u32[]{:S(2)}, u32[]{:S(2)}) collective-permute-start(f32[6,2,32]{1,0,2:T(8,128)S(1)} %get-tuple-element.68), channel_id=1, source_target_pairs={{0,1},{2,3},{4,5},{6,7},{8,9},{10,11},{12,13},{14,15},{16,17},{18,... | collective-permute-start | bytes 4616 | tf_op jit(solution)/shard_map/ppermute | solution.py:26
  52.7 7.0 %collective-permute-start.7 = (f32[6,2,32]{1,0,2:T(8,128)S(1)}, f32[6,2,32]{1,0,2:T(8,128)S(1)}, u32[]{:S(2)}, u32[]{:S(2)}) collective-permute-start(f32[6,2,32]{1,0,2:T(8,128)S(1)} %get-tuple-element.69), channel_id=1, source_target_pairs={{1,0},{3,2},{5,4},{7,6},{9,8},{11,10},{13,12},{15,14},{17,16},{19,... | collective-permute-start | bytes 4616 | tf_op jit(solution)/shard_map/ppermute | solution.py:27
  54.1 0.8 copy-start.5
  54.1 0.8 copy-start.6
  54.9 6.1 %collective-permute-start.2 = (f32[6,2,576]{2,1,0:T(2,128)}, f32[6,2,576]{2,1,0:T(2,128)}, u32[]{:S(2)}, u32[]{:S(2)}) collective-permute-start(f32[6,2,576]{2,1,0:T(2,128)} %get-tuple-element.54), channel_id=1, source_target_pairs={{0,1},{2,3},{4,5},{6,7},{8,9},{10,11},{12,13},{14,15},{16,17},{18,... | collective-permute-start | bytes 82952 | tf_op jit(solution)/shard_map/ppermute | solution.py:26
  58.5 3.4 %collective-permute-start.3 = (f32[6,2,576]{2,1,0:T(2,128)}, f32[6,2,576]{2,1,0:T(2,128)}, u32[]{:S(2)}, u32[]{:S(2)}) collective-permute-start(f32[6,2,576]{2,1,0:T(2,128)} %get-tuple-element.55), channel_id=1, source_target_pairs={{1,0},{3,2},{5,4},{7,6},{9,8},{11,10},{13,12},{15,14},{17,16},{19,... | collective-permute-start | bytes 82952 | tf_op jit(solution)/shard_map/ppermute | solution.py:27
  61.9 1.2 copy-start.22
  64.0 0.9 copy-start.11
  64.0 1.1 copy-start.12
  64.3 0.8 copy-start.25
  64.3 0.8 copy-start.24
  64.3 0.8 copy-start.23
  64.3 0.8 copy-start.20
  65.3 11.5 %collective-permute-start.8 = (f32[2,48,576]{2,1,0:T(8,128)S(1)}, f32[2,48,576]{2,1,0:T(8,128)S(1)}, u32[]{:S(2)}, u32[]{:S(2)}) collective-permute-start(f32[2,48,576]{2,1,0:T(8,128)S(1)} %get-tuple-element.46), channel_id=1, source_target_pairs={{0,2},{2,4},{4,6},{6,8},{8,10},{10,12},{12,14},{1,3},{3,5},{5,7},{... | collective-permute-start | bytes 663560 | tf_op jit(solution)/shard_map/ppermute | solution.py:26
  67.2 14.8 %collective-permute-start.9 = (f32[2,48,576]{2,1,0:T(8,128)S(1)}, f32[2,48,576]{2,1,0:T(8,128)S(1)}, u32[]{:S(2)}, u32[]{:S(2)}) collective-permute-start(f32[2,48,576]{2,1,0:T(8,128)S(1)} %get-tuple-element.46), channel_id=1, source_target_pairs={{2,0},{4,2},{6,4},{8,6},{10,8},{12,10},{14,12},{3,1},{5,3},{7,5},{... | collective-permute-start | bytes 663560 | tf_op jit(solution)/shard_map/ppermute | solution.py:27
  82.7 6.0 %collective-permute-start.10 = (f32[6,2,576]{2,1,0:T(2,128)}, f32[6,2,576]{2,1,0:T(2,128)}, u32[]{:S(2)}, u32[]{:S(2)}) collective-permute-start(f32[6,2,576]{2,1,0:T(2,128)} %get-tuple-element.52), channel_id=1, source_target_pairs={{0,1},{2,3},{4,5},{6,7},{8,9},{10,11},{12,13},{14,15},{16,17},{18,... | collective-permute-start | bytes 82952 | tf_op jit(solution)/shard_map/ppermute | solution.py:26
  85.3 3.4 %collective-permute-start.11 = (f32[6,2,576]{2,1,0:T(2,128)}, f32[6,2,576]{2,1,0:T(2,128)}, u32[]{:S(2)}, u32[]{:S(2)}) collective-permute-start(f32[6,2,576]{2,1,0:T(2,128)} %get-tuple-element.53), channel_id=1, source_target_pairs={{1,0},{3,2},{5,4},{7,6},{9,8},{11,10},{13,12},{15,14},{17,16},{19,... | collective-permute-start | bytes 82952 | tf_op jit(solution)/shard_map/ppermute | solution.py:27
  90.2 0.9 copy-start.10
  91.3 11.0 %collective-permute-start.12 = (f32[2,48,576]{2,1,0:T(8,128)S(1)}, f32[2,48,576]{2,1,0:T(8,128)S(1)}, u32[]{:S(2)}, u32[]{:S(2)}) collective-permute-start(f32[2,48,576]{2,1,0:T(8,128)S(1)} %get-tuple-element.44), channel_id=1, source_target_pairs={{0,2},{2,4},{4,6},{6,8},{8,10},{10,12},{12,14},{1,3},{3,5},{5,7},{... | collective-permute-start | bytes 663560 | tf_op jit(solution)/shard_map/ppermute | solution.py:26
  93.2 14.9 %collective-permute-start.13 = (f32[2,48,576]{2,1,0:T(8,128)S(1)}, f32[2,48,576]{2,1,0:T(8,128)S(1)}, u32[]{:S(2)}, u32[]{:S(2)}) collective-permute-start(f32[2,48,576]{2,1,0:T(8,128)S(1)} %get-tuple-element.44), channel_id=1, source_target_pairs={{2,0},{4,2},{6,4},{8,6},{10,8},{12,10},{14,12},{3,1},{5,3},{7,5},{... | collective-permute-start | bytes 663560 | tf_op jit(solution)/shard_map/ppermute | solution.py:27
  108.8 4.9 %collective-permute-start.14 = (f32[6,2,576]{2,1,0:T(2,128)}, f32[6,2,576]{2,1,0:T(2,128)S(1)}, u32[]{:S(2)}, u32[]{:S(2)}) collective-permute-start(f32[6,2,576]{2,1,0:T(2,128)} %get-tuple-element.50), channel_id=1, source_target_pairs={{0,1},{2,3},{4,5},{6,7},{8,9},{10,11},{12,13},{14,15},{16,17},{18,... | collective-permute-start | bytes 82952 | tf_op jit(solution)/shard_map/ppermute | solution.py:26
  110.9 3.2 %copy-start.8 = (f32[2,48,576]{2,1,0:T(8,128)S(1)}, f32[2,48,576]{2,1,0:T(8,128)}, u32[]{:S(2)}) copy-start(f32[2,48,576]{2,1,0:T(8,128)} %copy-done.7) | copy-start | bytes 663556
  110.9 3.2 %collective-permute-start.15 = (f32[6,2,576]{2,1,0:T(2,128)S(1)}, f32[6,2,576]{2,1,0:T(2,128)S(1)}, u32[]{:S(2)}, u32[]{:S(2)}) collective-permute-start(f32[6,2,576]{2,1,0:T(2,128)S(1)} %get-tuple-element.51), channel_id=1, source_target_pairs={{1,0},{3,2},{5,4},{7,6},{9,8},{11,10},{13,12},{15,14},{17,16},{19,... | collective-permute-start | bytes 82952 | tf_op jit(solution)/shard_map/ppermute | solution.py:27
  114.8 1.0 copy-start.4
  115.0 1.4 copy-start.3
  125.7 23.4 %copy-start.15 = (f32[2,48,20]{1,0,2:T(2,128)}, f32[2,48,20]{1,0,2:T(2,128)S(1)}, u32[]{:S(2)}) copy-start(f32[2,48,20]{1,0,2:T(2,128)S(1)} %reshape.208) | copy-start | bytes 23044
  125.8 23.3 %copy-start.16 = (f32[2,48,20]{1,0,2:T(2,128)}, f32[2,48,20]{1,0,2:T(2,128)S(1)}, u32[]{:S(2)}) copy-start(f32[2,48,20]{1,0,2:T(2,128)S(1)} %reshape.209) | copy-start | bytes 23044
  130.3 4.5 %copy-start.14 = (f32[40,20]{0,1:T(8,128)S(1)}, f32[40,20]{0,1:T(8,128)}, u32[]{:S(2)}) copy-start(f32[40,20]{0,1:T(8,128)} %param.23) | copy-start | bytes 9604
  135.2 5.9 %collective-permute-start.20 = (f32[1,48,40]{1,2,0:T(8,128)S(1)}, f32[1,48,40]{1,2,0:T(8,128)S(1)}, u32[]{:S(2)}, u32[]{:S(2)}) collective-permute-start(f32[1,48,40]{1,2,0:T(8,128)S(1)} %get-tuple-element.79), channel_id=1, source_target_pairs={{2,0},{4,2},{6,4},{8,6},{10,8},{12,10},{14,12},{3,1},{5,3},{7,5},{... | collective-permute-start | bytes 23048 | tf_op jit(solution)/shard_map/ppermute | solution.py:27
  137.1 6.6 %collective-permute-start.21 = (f32[1,48,40]{1,2,0:T(8,128)S(1)}, f32[1,48,40]{1,2,0:T(8,128)S(1)}, u32[]{:S(2)}, u32[]{:S(2)}) collective-permute-start(f32[1,48,40]{1,2,0:T(8,128)S(1)} %get-tuple-element.78), channel_id=1, source_target_pairs={{0,2},{2,4},{4,6},{6,8},{8,10},{10,12},{12,14},{1,3},{3,5},{5,7},{... | collective-permute-start | bytes 23048 | tf_op jit(solution)/shard_map/ppermute | solution.py:26
  143.8 4.3 %collective-permute-start.22 = (f32[4,1,40]{1,2,0:T(8,128)S(1)}, f32[4,1,40]{1,2,0:T(8,128)S(1)}, u32[]{:S(2)}, u32[]{:S(2)}) collective-permute-start(f32[4,1,40]{1,2,0:T(8,128)S(1)} %get-tuple-element.72), channel_id=1, source_target_pairs={{1,0},{3,2},{5,4},{7,6},{9,8},{11,10},{13,12},{15,14},{17,16},{19,... | collective-permute-start | bytes 1928 | tf_op jit(solution)/shard_map/ppermute | solution.py:27
  145.1 3.9 %collective-permute-start.23 = (f32[4,1,40]{1,2,0:T(8,128)S(1)}, f32[4,1,40]{1,2,0:T(8,128)S(1)}, u32[]{:S(2)}, u32[]{:S(2)}) collective-permute-start(f32[4,1,40]{1,2,0:T(8,128)S(1)} %get-tuple-element.73), channel_id=1, source_target_pairs={{0,1},{2,3},{4,5},{6,7},{8,9},{10,11},{12,13},{14,15},{16,17},{18,... | collective-permute-start | bytes 1928 | tf_op jit(solution)/shard_map/ppermute | solution.py:26
  (7 other events, 4.8 us)
where the time goes:
time: 161 us; the launch traced here: 160 us
  starting transfers between devices  64.3 us (40%)
  blocking collectives  35.2 us (22%)
  waiting for transfers between devices  23.1 us (14%)
  other arithmetic  13.4 us (8%)
  local copies, waits for them, and re-layouts  12.4 us (8%)
  matrix products  9.09 us (6%)
  between operations  2.19 us (1%)
    ppermute x12, starting transfers between devices, extended(): before = lax.ppermute(last, axis, up)  34 us
    ppermute x12, starting transfers between devices, extended(): after = lax.ppermute(leading, axis, down)  30.3 us
    ppermute x12, waiting for transfers between devices, extended(): after = lax.ppermute(leading, axis, down)  12.4 us
    ppermute x12, waiting for transfers between devices, extended(): before = lax.ppermute(last, axis, up)  10.7 us
    all_gather x2, blocking collectives, body(): lax.all_gather(first_u, 'grp', axis=2, tiled=True)  8.9 us
    all_gather x2, blocking collectives, body(): lax.all_gather(first_v, 'grp', axis=2, tiled=True)  8.9 us
    unnamed x1, blocking collectives  8.49 us
    unnamed x70, local copies, waits for them, and re-layouts  7.46 us
  transfers between devices with their start and end apart: 24, of which 8 were waited for; matrix products, arithmetic and copies ran while one was open for 11% of the time, Pallas kernels for 0%

commit v1 on v0

--- a/solution.py
+++ b/solution.py
@@ -14,6 +14,27 @@
 ocean_step = 0.4
 coriolis = 0.5
 viscosity = 0.1
+
+
+def laid_out(pieces, dim):
+    dims = list(pieces.shape[1:])
+    dims[dim] *= pieces.shape[0]
+    return jnp.moveaxis(pieces, 0, dim).reshape(dims)
+
+
+def grow_blocks(value, axis):
+    size, position = (lax.axis_size(axis), lax.axis_index(axis))
+    blocks, bit = (value[None], 1)
+    while bit < size:
+        other = lax.ppermute(blocks, axis, [(i, i ^ bit) for i in range(size)])
+        low = position & bit == 0
+        blocks = jnp.concatenate([jnp.where(low, blocks, other), jnp.where(low, other, blocks)])
+        bit *= 2
+    return blocks
+
+
+def collect(shard, axis, dim):
+    return laid_out(grow_blocks(shard, axis), dim)
 
 
 def extended(array, sides, width):
@@ -156,7 +177,7 @@
         )
         whole_u, whole_v = (
             lax.all_gather(first_u, "grp", axis=2, tiled=True),
-            lax.all_gather(first_v, "grp", axis=2, tiled=True),
+            collect(first_v, "grp", 2),
         )
         velocity_u = wet_factor * (
             first_u + jnp.einsum("abk,kl->abl", whole_u, mixing, precision=highest)

time: 161 us -> 155 us (0.963)
  blocking collectives: 35.2 us -> 26.3 us
  waiting for transfers between devices: 23.1 us -> 26.9 us
    all_gather x2 -> x0, blocking collectives: 8.9 us -> none  [body(): lax.all_gather(first_v, 'grp', axis=2, tiled=True)]
    ppermute x0 -> x2, waiting for transfers between devices: none -> 3.12 us  [grow_blocks(): other = lax.ppermute(blocks, axis, [(i, i ^ bit) for i in range(size)])]
    ppermute x12, starting transfers between devices: 34 us -> 32.1 us  [extended(): before = lax.ppermute(last, axis, up)]
  transfers between devices with their start and end apart: 24 -> 26, of which waited for: 8 -> 10; matrix products, arithmetic and copies ran while one was open for 11% -> 12% of each run, Pallas kernels for 0% -> 0%
where the time goes in v1:
time: 155 us; the launch traced here: 153 us
  starting transfers between devices  63.6 us (41%)
  waiting for transfers between devices  26.9 us (17%)
  blocking collectives  26.3 us (17%)
  other arithmetic  13.3 us (9%)
  local copies, waits for them, and re-layouts  11.8 us (8%)
  matrix products  9.14 us (6%)
  between operations  2.21 us (1%)
    ppermute x12, starting transfers between devices, extended(): before = lax.ppermute(last, axis, up)  32.1 us
    ppermute x12, starting transfers between devices, extended(): after = lax.ppermute(leading, axis, down)  30.3 us
    ppermute x12, waiting for transfers between devices, extended(): after = lax.ppermute(leading, axis, down)  13.1 us
    ppermute x12, waiting for transfers between devices, extended(): before = lax.ppermute(last, axis, up)  10.7 us
    all_gather x2, blocking collectives, body(): lax.all_gather(first_u, 'grp', axis=2, tiled=True)  8.9 us
    unnamed x1, blocking collectives  8.48 us
    unnamed x70, local copies, waits for them, and re-layouts  7.47 us
    concatenate x7, other arithmetic, extended(): array = jnp.concatenate([before, array, after], axis=dim)  4.84 us
  transfers between devices with their start and end apart: 26, of which 10 were waited for; matrix products, arithmetic and copies ran while one was open for 12% of the time, Pallas kernels for 0%

profile of v1, /device:TPU:24, one launch (start us, length us, event | category | flops | bytes accessed | tf_op | source)
XLA Modules:
  0.0 153.2 jit_solution(15306382402794167509)
XLA Ops:
  1.5 4.5 %all_gather.12 = f32[2,48,40]{1,0,2:T(2,128)S(1)} all-gather(f32[2,48,20]{1,0,2:T(2,128)S(1)} %copy-done.17), channel_id=1, replica_groups=mesh['grp'=2,'gx'=8,'gy'=2] {'grp'}, dimensions={2}, use_global_device_ids=true | all-gather | bytes 23040 | tf_op jit(solution)/shard_map/all_gather | solution.py:102
  7.9 4.4 %all_gather.13 = f32[2,48,40]{1,0,2:T(2,128)S(1)} all-gather(f32[2,48,20]{1,0,2:T(2,128)S(1)} %copy-done.18), channel_id=1, replica_groups=mesh['grp'=2,'gx'=8,'gy'=2] {'grp'}, dimensions={2}, use_global_device_ids=true | all-gather | bytes 23040 | tf_op jit(solution)/shard_map/all_gather | solution.py:103
  13.4 3.4 %collective-permute-start.4 = (f32[2,48,32]{1,0,2:T(2,128)S(1)}, f32[2,48,32]{1,0,2:T(2,128)}, u32[]{:S(2)}, u32[]{:S(2)}) collective-permute-start(f32[2,48,32]{1,0,2:T(2,128)S(1)} %constant_dynamic-update-slice_fusion), channel_id=1, source_target_pairs={{0,2},{2,4},{4,6},{6,8},{8,10},{10,12},{12,14},{1,3},{3,5},{5,7},{... | collective-permute-start | bytes 36872 | tf_op jit(solution)/shard_map/ppermute | solution.py:47
  16.8 3.3 %collective-permute-start.5 = (f32[2,48,32]{1,0,2:T(2,128)S(1)}, f32[2,48,32]{1,0,2:T(2,128)}, u32[]{:S(2)}, u32[]{:S(2)}) collective-permute-start(f32[2,48,32]{1,0,2:T(2,128)S(1)} %constant_dynamic-update-slice_fusion), channel_id=1, source_target_pairs={{2,0},{4,2},{6,4},{8,6},{10,8},{12,10},{14,12},{3,1},{5,3},{7,5},{... | collective-permute-start | bytes 36872 | tf_op jit(solution)/shard_map/ppermute | solution.py:48
  20.8 3.2 %collective-permute-start = (f32[2,48,576]{2,1,0:T(8,128)S(1)}, f32[2,48,576]{2,1,0:T(8,128)S(1)}, u32[]{:S(2)}, u32[]{:S(2)}) collective-permute-start(f32[2,48,576]{2,1,0:T(8,128)S(1)} %get-tuple-element.49), channel_id=1, source_target_pairs={{0,2},{2,4},{4,6},{6,8},{8,10},{10,12},{12,14},{1,3},{3,5},{5,7},{... | collective-permute-start | bytes 663560 | tf_op jit(solution)/shard_map/ppermute | solution.py:47
  24.6 3.6 %collective-permute-start.16 = (f32[1,48,40]{1,2,0:T(8,128)}, f32[1,48,40]{1,2,0:T(8,128)}, u32[]{:S(2)}, u32[]{:S(2)}) collective-permute-start(f32[1,48,40]{1,2,0:T(8,128)} %get-tuple-element.85), channel_id=1, source_target_pairs={{2,0},{4,2},{6,4},{8,6},{10,8},{12,10},{14,12},{3,1},{5,3},{7,5},{... | collective-permute-start | bytes 23048 | tf_op jit(solution)/shard_map/ppermute | solution.py:48
  28.3 2.8 %collective-permute-start.17 = (f32[1,48,40]{1,2,0:T(8,128)}, f32[1,48,40]{1,2,0:T(8,128)}, u32[]{:S(2)}, u32[]{:S(2)}) collective-permute-start(f32[1,48,40]{1,2,0:T(8,128)} %get-tuple-element.84), channel_id=1, source_target_pairs={{0,2},{2,4},{4,6},{6,8},{8,10},{10,12},{12,14},{1,3},{3,5},{5,7},{... | collective-permute-start | bytes 23048 | tf_op jit(solution)/shard_map/ppermute | solution.py:47
  32.7 1.2 convolution_multiply_fusion.2
  33.9 0.9 broadcast_multiply_fusion
  35.7 0.9 copy.305
  37.5 1.3 collective-permute-start.18
  38.8 3.0 %collective-permute-start.19 = (f32[4,1,40]{1,2,0:T(8,128)S(1)}, f32[4,1,40]{1,2,0:T(8,128)S(1)}, u32[]{:S(2)}, u32[]{:S(2)}) collective-permute-start(f32[4,1,40]{1,2,0:T(8,128)S(1)} %get-tuple-element.77), channel_id=1, source_target_pairs={{0,1},{2,3},{4,5},{6,7},{8,9},{10,11},{12,13},{14,15},{16,17},{18,... | collective-permute-start | bytes 1928 | tf_op jit(solution)/shard_map/ppermute | solution.py:47
  43.8 4.0 %collective-permute-start.1 = (f32[2,48,576]{2,1,0:T(8,128)S(1)}, f32[2,48,576]{2,1,0:T(8,128)S(1)}, u32[]{:S(2)}, u32[]{:S(2)}) collective-permute-start(f32[2,48,576]{2,1,0:T(8,128)S(1)} %get-tuple-element.49), channel_id=1, source_target_pairs={{2,0},{4,2},{6,4},{8,6},{10,8},{12,10},{14,12},{3,1},{5,3},{7,5},{... | collective-permute-start | bytes 663560 | tf_op jit(solution)/shard_map/ppermute | solution.py:48
  47.7 0.9 fusion.41
  49.6 1.3 collective-permute-start.6
  50.9 1.3 collective-permute-start.7
  53.6 3.0 %collective-permute-start.2 = (f32[6,2,576]{2,1,0:T(2,128)}, f32[6,2,576]{2,1,0:T(2,128)}, u32[]{:S(2)}, u32[]{:S(2)}) collective-permute-start(f32[6,2,576]{2,1,0:T(2,128)} %get-tuple-element.54), channel_id=1, source_target_pairs={{0,1},{2,3},{4,5},{6,7},{8,9},{10,11},{12,13},{14,15},{16,17},{18,... | collective-permute-start | bytes 82952 | tf_op jit(solution)/shard_map/ppermute | solution.py:47
  56.6 1.3 collective-permute-start.3
  57.9 0.9 pad_maximum_fusion.41
  59.1 0.9 collective-permute-done.3
  60.1 1.2 pad_maximum_fusion
  63.4 1.9 %collective-permute-start.8 = (f32[2,48,576]{2,1,0:T(8,128)S(1)}, f32[2,48,576]{2,1,0:T(8,128)S(1)}, u32[]{:S(2)}, u32[]{:S(2)}) collective-permute-start(f32[2,48,576]{2,1,0:T(8,128)S(1)} %get-tuple-element.46), channel_id=1, source_target_pairs={{0,2},{2,4},{4,6},{6,8},{8,10},{10,12},{12,14},{1,3},{3,5},{5,7},{... | collective-permute-start | bytes 663560 | tf_op jit(solution)/shard_map/ppermute | solution.py:47
  65.4 4.8 %collective-permute-start.9 = (f32[2,48,576]{2,1,0:T(8,128)S(1)}, f32[2,48,576]{2,1,0:T(8,128)S(1)}, u32[]{:S(2)}, u32[]{:S(2)}) collective-permute-start(f32[2,48,576]{2,1,0:T(8,128)S(1)} %get-tuple-element.46), channel_id=1, source_target_pairs={{2,0},{4,2},{6,4},{8,6},{10,8},{12,10},{14,12},{3,1},{5,3},{7,5},{... | collective-permute-start | bytes 663560 | tf_op jit(solution)/shard_map/ppermute | solution.py:48
  70.2 0.9 fusion.119
  71.1 3.8 %collective-permute-done.8 = f32[2,48,576]{2,1,0:T(8,128)S(1)} collective-permute-done((f32[2,48,576]{2,1,0:T(8,128)S(1)}, f32[2,48,576]{2,1,0:T(8,128)S(1)}, u32[]{:S(2)}, u32[]{:S(2)}) %collective-permute-start.8) | collective-permute-done | bytes 221216 | tf_op jit(solution)/shard_map/ppermute | solution.py:47
  75.0 5.2 %collective-permute-done.9 = f32[2,48,576]{2,1,0:T(8,128)S(1)} collective-permute-done((f32[2,48,576]{2,1,0:T(8,128)S(1)}, f32[2,48,576]{2,1,0:T(8,128)S(1)}, u32[]{:S(2)}, u32[]{:S(2)}) %collective-permute-start.9) | collective-permute-done | bytes 221216 | tf_op jit(solution)/shard_map/ppermute | solution.py:48
  80.8 2.6 %collective-permute-start.10 = (f32[6,2,576]{2,1,0:T(2,128)}, f32[6,2,576]{2,1,0:T(2,128)}, u32[]{:S(2)}, u32[]{:S(2)}) collective-permute-start(f32[6,2,576]{2,1,0:T(2,128)} %get-tuple-element.52), channel_id=1, source_target_pairs={{0,1},{2,3},{4,5},{6,7},{8,9},{10,11},{12,13},{14,15},{16,17},{18,... | collective-permute-start | bytes 82952 | tf_op jit(solution)/shard_map/ppermute | solution.py:47
  83.4 1.3 collective-permute-start.11
  84.7 2.1 %convolution_multiply_fusion.1 = f32[96,576]{1,0:T(8,128)} fusion(bf16[512,576]{0,1:T(8,128)(2,1)S(1)} %copy-done, f32[96,512]{1,0:T(8,128)} %fusion.119, bf16[96,576]{1,0:T(8,128)(2,1)S(1)} %bitcast.77, bf16[576,512]{1,0:T(8,128)(2,1)S(1)} %copy-done.2), kind=kOutput, calls=%fused_computation.3 | convolution fusion | flops 113399808 | bytes 1708032 | tf_op jit(solution)/shard_map/dot_general | solution.py:131
  86.9 1.1 pad_maximum_fusion.1
  89.5 1.9 %collective-permute-start.12 = (f32[2,48,576]{2,1,0:T(8,128)S(1)}, f32[2,48,576]{2,1,0:T(8,128)S(1)}, u32[]{:S(2)}, u32[]{:S(2)}) collective-permute-start(f32[2,48,576]{2,1,0:T(8,128)S(1)} %get-tuple-element.44), channel_id=1, source_target_pairs={{0,2},{2,4},{4,6},{6,8},{8,10},{10,12},{12,14},{1,3},{3,5},{5,7},{... | collective-permute-start | bytes 663560 | tf_op jit(solution)/shard_map/ppermute | solution.py:47
  91.4 4.8 %collective-permute-start.13 = (f32[2,48,576]{2,1,0:T(8,128)S(1)}, f32[2,48,576]{2,1,0:T(8,128)S(1)}, u32[]{:S(2)}, u32[]{:S(2)}) collective-permute-start(f32[2,48,576]{2,1,0:T(8,128)S(1)} %get-tuple-element.44), channel_id=1, source_target_pairs={{2,0},{4,2},{6,4},{8,6},{10,8},{12,10},{14,12},{3,1},{5,3},{7,5},{... | collective-permute-start | bytes 663560 | tf_op jit(solution)/shard_map/ppermute | solution.py:48
  96.2 0.9 fusion.120
  97.2 3.3 %collective-permute-done.12 = f32[2,48,576]{2,1,0:T(8,128)S(1)} collective-permute-done((f32[2,48,576]{2,1,0:T(8,128)S(1)}, f32[2,48,576]{2,1,0:T(8,128)S(1)}, u32[]{:S(2)}, u32[]{:S(2)}) %collective-permute-start.12) | collective-permute-done | bytes 221216 | tf_op jit(solution)/shard_map/ppermute | solution.py:47
  100.5 5.8 %collective-permute-done.13 = f32[2,48,576]{2,1,0:T(8,128)S(1)} collective-permute-done((f32[2,48,576]{2,1,0:T(8,128)S(1)}, f32[2,48,576]{2,1,0:T(8,128)S(1)}, u32[]{:S(2)}, u32[]{:S(2)}) %collective-permute-start.13) | collective-permute-done | bytes 221216 | tf_op jit(solution)/shard_map/ppermute | solution.py:48
  107.0 2.0 %collective-permute-start.14 = (f32[6,2,576]{2,1,0:T(2,128)}, f32[6,2,576]{2,1,0:T(2,128)S(1)}, u32[]{:S(2)}, u32[]{:S(2)}) collective-permute-start(f32[6,2,576]{2,1,0:T(2,128)} %get-tuple-element.50), channel_id=1, source_target_pairs={{0,1},{2,3},{4,5},{6,7},{8,9},{10,11},{12,13},{14,15},{16,17},{18,... | collective-permute-start | bytes 82952 | tf_op jit(solution)/shard_map/ppermute | solution.py:47
  109.0 1.4 collective-permute-start.15
  110.5 1.4 convolution_multiply_fusion
  115.2 8.5 %all-reduce.2 = (f32[96,40]{0,1:T(8,128)S(1)}, f32[96,40]{0,1:T(8,128)S(1)}) all-reduce(f32[96,40]{0,1:T(8,128)S(1)} %fusion.121, f32[96,40]{0,1:T(8,128)S(1)} %fusion.122), channel_id=2, replica_groups=mesh['grp'=2,'gx'=8,'gy'=2] {'grp'}, use_global_device_ids=true, to_apply=%region_0.2.clone | all-reduce | flops 7680 | bytes 61440
  124.0 4.5 %all_gather.14 = f32[2,48,40]{1,0,2:T(2,128)S(1)} all-gather(f32[2,48,20]{1,0,2:T(2,128)S(1)} %copy.312), channel_id=1, replica_groups=mesh['grp'=2,'gx'=8,'gy'=2] {'grp'}, dimensions={2}, use_global_device_ids=true | all-gather | bytes 23040 | tf_op jit(solution)/shard_map/all_gather | solution.py:179
  129.2 3.1 %collective-permute-done.20 = f32[1,2,48,20]{2,3,1,0:T(8,128)S(1)} collective-permute-done((f32[1,2,48,20]{2,3,1,0:T(8,128)S(1)}, f32[1,2,48,20]{2,3,1,0:T(8,128)S(1)}, u32[]{:S(2)}, u32[]{:S(2)}) %collective-permute-start.20) | collective-permute-done | bytes 7712 | tf_op jit(solution)/shard_map/ppermute | solution.py:29
  132.5 1.9 %collective-permute-start.21 = (f32[1,48,40]{1,2,0:T(8,128)S(1)}, f32[1,48,40]{1,2,0:T(8,128)S(1)}, u32[]{:S(2)}, u32[]{:S(2)}) collective-permute-start(f32[1,48,40]{1,2,0:T(8,128)S(1)} %get-tuple-element.81), channel_id=1, source_target_pairs={{2,0},{4,2},{6,4},{8,6},{10,8},{12,10},{14,12},{3,1},{5,3},{7,5},{... | collective-permute-start | bytes 23048 | tf_op jit(solution)/shard_map/ppermute | solution.py:48
  134.5 3.9 %collective-permute-start.22 = (f32[1,48,40]{1,2,0:T(8,128)S(1)}, f32[1,48,40]{1,2,0:T(8,128)S(1)}, u32[]{:S(2)}, u32[]{:S(2)}) collective-permute-start(f32[1,48,40]{1,2,0:T(8,128)S(1)} %get-tuple-element.80), channel_id=1, source_target_pairs={{0,2},{2,4},{4,6},{6,8},{8,10},{10,12},{12,14},{1,3},{3,5},{5,7},{... | collective-permute-start | bytes 23048 | tf_op jit(solution)/shard_map/ppermute | solution.py:47
  138.4 2.6 %collective-permute-done.22 = f32[1,48,40]{1,2,0:T(8,128)S(1)} collective-permute-done((f32[1,48,40]{1,2,0:T(8,128)S(1)}, f32[1,48,40]{1,2,0:T(8,128)S(1)}, u32[]{:S(2)}, u32[]{:S(2)}) %collective-permute-start.22) | collective-permute-done | bytes 7712 | tf_op jit(solution)/shard_map/ppermute | solution.py:47
  141.1 1.3 collective-permute-start.23
  142.4 3.0 %collective-permute-start.24 = (f32[4,1,40]{1,2,0:T(8,128)S(1)}, f32[4,1,40]{1,2,0:T(8,128)S(1)}, u32[]{:S(2)}, u32[]{:S(2)}) collective-permute-start(f32[4,1,40]{1,2,0:T(8,128)S(1)} %get-tuple-element.73), channel_id=1, source_target_pairs={{0,1},{2,3},{4,5},{6,7},{8,9},{10,11},{12,13},{14,15},{16,17},{18,... | collective-permute-start | bytes 1928 | tf_op jit(solution)/shard_map/ppermute | solution.py:47
  145.5 0.9 collective-permute-done.24
  147.2 4.5 %all_gather.15 = f32[2,48,40]{1,0,2:T(2,128)S(1)} all-gather(f32[2,48,20]{1,0,2:T(2,128)S(1)} %copy.320), channel_id=1, replica_groups=mesh['grp'=2,'gx'=8,'gy'=2] {'grp'}, dimensions={2}, use_global_device_ids=true | all-gather | bytes 23040 | tf_op jit(solution)/shard_map/all_gather | solution.py:179
  (165 shorter events, 24.2 us)
Async XLA Ops:
  0.6 32.1 %copy-start = (bf16[512,576]{0,1:T(8,128)(2,1)S(1)}, bf16[512,576]{0,1:T(8,128)(2,1)}, u32[]{:S(2)}) copy-start(bf16[512,576]{0,1:T(8,128)(2,1)} %param.22) | copy-start | bytes 1769476
  0.7 0.8 copy-start.17
  12.4 7.8 %copy-start.28 = (s32[2,48]{1,0:T(2,128)S(1)}, s32[2,48]{1,0:T(2,128)}, u32[]{:S(2)}) copy-start(s32[2,48]{1,0:T(2,128)} %param.14) | copy-start | bytes 1156
  12.4 7.8 %copy-start.13 = (f32[2,48,576]{2,1,0:T(8,128)S(1)}, f32[2,48,576]{2,1,0:T(8,128)}, u32[]{:S(2)}) copy-start(f32[2,48,576]{2,1,0:T(8,128)} %param.13) | copy-start | bytes 663556
  13.0 19.5 %copy-start.1 = (bf16[576,512]{1,0:T(8,128)(2,1)S(1)}, bf16[576,512]{1,0:T(8,128)(2,1)}, u32[]{:S(2)}) copy-start(bf16[576,512]{1,0:T(8,128)(2,1)} %param.20) | copy-start | bytes 1769476
  13.4 35.2 %collective-permute-start.4 = (f32[2,48,32]{1,0,2:T(2,128)S(1)}, f32[2,48,32]{1,0,2:T(2,128)}, u32[]{:S(2)}, u32[]{:S(2)}) collective-permute-start(f32[2,48,32]{1,0,2:T(2,128)S(1)} %constant_dynamic-update-slice_fusion), channel_id=1, source_target_pairs={{0,2},{2,4},{4,6},{6,8},{8,10},{10,12},{12,14},{1,3},{3,5},{5,7},{... | collective-permute-start | bytes 36872 | tf_op jit(solution)/shard_map/ppermute | solution.py:47
  16.8 31.8 %collective-permute-start.5 = (f32[2,48,32]{1,0,2:T(2,128)S(1)}, f32[2,48,32]{1,0,2:T(2,128)}, u32[]{:S(2)}, u32[]{:S(2)}) collective-permute-start(f32[2,48,32]{1,0,2:T(2,128)S(1)} %constant_dynamic-update-slice_fusion), channel_id=1, source_target_pairs={{2,0},{4,2},{6,4},{8,6},{10,8},{12,10},{14,12},{3,1},{5,3},{7,5},{... | collective-permute-start | bytes 36872 | tf_op jit(solution)/shard_map/ppermute | solution.py:48
  20.2 12.3 %copy-start.27 = (f32[40,32]{0,1:T(8,128)S(1)}, f32[40,32]{0,1:T(8,128)}, u32[]{:S(2)}) copy-start(f32[40,32]{0,1:T(8,128)} %param.19) | copy-start | bytes 15364
  20.8 12.0 %copy-start.2 = (bf16[576,512]{1,0:T(8,128)(2,1)S(1)}, bf16[576,512]{1,0:T(8,128)(2,1)}, u32[]{:S(2)}) copy-start(bf16[576,512]{1,0:T(8,128)(2,1)} %param.21) | copy-start | bytes 1769476
  20.8 31.4 %collective-permute-start = (f32[2,48,576]{2,1,0:T(8,128)S(1)}, f32[2,48,576]{2,1,0:T(8,128)S(1)}, u32[]{:S(2)}, u32[]{:S(2)}) collective-permute-start(f32[2,48,576]{2,1,0:T(8,128)S(1)} %get-tuple-element.49), channel_id=1, source_target_pairs={{0,2},{2,4},{4,6},{6,8},{8,10},{10,12},{12,14},{1,3},{3,5},{5,7},{... | collective-permute-start | bytes 663560 | tf_op jit(solution)/shard_map/ppermute | solution.py:47
  24.6 12.0 %collective-permute-start.16 = (f32[1,48,40]{1,2,0:T(8,128)}, f32[1,48,40]{1,2,0:T(8,128)}, u32[]{:S(2)}, u32[]{:S(2)}) collective-permute-start(f32[1,48,40]{1,2,0:T(8,128)} %get-tuple-element.85), channel_id=1, source_target_pairs={{2,0},{4,2},{6,4},{8,6},{10,8},{12,10},{14,12},{3,1},{5,3},{7,5},{... | collective-permute-start | bytes 23048 | tf_op jit(solution)/shard_map/ppermute | solution.py:48
  28.3 8.4 %collective-permute-start.17 = (f32[1,48,40]{1,2,0:T(8,128)}, f32[1,48,40]{1,2,0:T(8,128)}, u32[]{:S(2)}, u32[]{:S(2)}) collective-permute-start(f32[1,48,40]{1,2,0:T(8,128)} %get-tuple-element.84), channel_id=1, source_target_pairs={{0,2},{2,4},{4,6},{6,8},{8,10},{10,12},{12,14},{1,3},{3,5},{5,7},{... | collective-permute-start | bytes 23048 | tf_op jit(solution)/shard_map/ppermute | solution.py:47
  37.5 6.2 %collective-permute-start.18 = (f32[4,1,40]{1,2,0:T(8,128)S(1)}, f32[4,1,40]{1,2,0:T(8,128)S(1)}, u32[]{:S(2)}, u32[]{:S(2)}) collective-permute-start(f32[4,1,40]{1,2,0:T(8,128)S(1)} %get-tuple-element.76), channel_id=1, source_target_pairs={{1,0},{3,2},{5,4},{7,6},{9,8},{11,10},{13,12},{15,14},{17,16},{19,... | collective-permute-start | bytes 1928 | tf_op jit(solution)/shard_map/ppermute | solution.py:48
  38.8 8.9 %collective-permute-start.19 = (f32[4,1,40]{1,2,0:T(8,128)S(1)}, f32[4,1,40]{1,2,0:T(8,128)S(1)}, u32[]{:S(2)}, u32[]{:S(2)}) collective-permute-start(f32[4,1,40]{1,2,0:T(8,128)S(1)} %get-tuple-element.77), channel_id=1, source_target_pairs={{0,1},{2,3},{4,5},{6,7},{8,9},{10,11},{12,13},{14,15},{16,17},{18,... | collective-permute-start | bytes 1928 | tf_op jit(solution)/shard_map/ppermute | solution.py:47
  43.8 9.1 %collective-permute-start.1 = (f32[2,48,576]{2,1,0:T(8,128)S(1)}, f32[2,48,576]{2,1,0:T(8,128)S(1)}, u32[]{:S(2)}, u32[]{:S(2)}) collective-permute-start(f32[2,48,576]{2,1,0:T(8,128)S(1)} %get-tuple-element.49), channel_id=1, source_target_pairs={{2,0},{4,2},{6,4},{8,6},{10,8},{12,10},{14,12},{3,1},{5,3},{7,5},{... | collective-permute-start | bytes 663560 | tf_op jit(solution)/shard_map/ppermute | solution.py:48
  49.6 8.4 %collective-permute-start.6 = (f32[6,2,32]{1,0,2:T(8,128)S(1)}, f32[6,2,32]{1,0,2:T(8,128)S(1)}, u32[]{:S(2)}, u32[]{:S(2)}) collective-permute-start(f32[6,2,32]{1,0,2:T(8,128)S(1)} %get-tuple-element.68), channel_id=1, source_target_pairs={{0,1},{2,3},{4,5},{6,7},{8,9},{10,11},{12,13},{14,15},{16,17},{18,... | collective-permute-start | bytes 4616 | tf_op jit(solution)/shard_map/ppermute | solution.py:47
  50.9 7.1 %collective-permute-start.7 = (f32[6,2,32]{1,0,2:T(8,128)S(1)}, f32[6,2,32]{1,0,2:T(8,128)S(1)}, u32[]{:S(2)}, u32[]{:S(2)}) collective-permute-start(f32[6,2,32]{1,0,2:T(8,128)S(1)} %get-tuple-element.69), channel_id=1, source_target_pairs={{1,0},{3,2},{5,4},{7,6},{9,8},{11,10},{13,12},{15,14},{17,16},{19,... | collective-permute-start | bytes 4616 | tf_op jit(solution)/shard_map/ppermute | solution.py:48
  52.2 1.4 copy-start.5
  53.6 5.5 %collective-permute-start.2 = (f32[6,2,576]{2,1,0:T(2,128)}, f32[6,2,576]{2,1,0:T(2,128)}, u32[]{:S(2)}, u32[]{:S(2)}) collective-permute-start(f32[6,2,576]{2,1,0:T(2,128)} %get-tuple-element.54), channel_id=1, source_target_pairs={{0,1},{2,3},{4,5},{6,7},{8,9},{10,11},{12,13},{14,15},{16,17},{18,... | collective-permute-start | bytes 82952 | tf_op jit(solution)/shard_map/ppermute | solution.py:47
  56.6 3.4 %collective-permute-start.3 = (f32[6,2,576]{2,1,0:T(2,128)}, f32[6,2,576]{2,1,0:T(2,128)}, u32[]{:S(2)}, u32[]{:S(2)}) collective-permute-start(f32[6,2,576]{2,1,0:T(2,128)} %get-tuple-element.55), channel_id=1, source_target_pairs={{1,0},{3,2},{5,4},{7,6},{9,8},{11,10},{13,12},{15,14},{17,16},{19,... | collective-permute-start | bytes 82952 | tf_op jit(solution)/shard_map/ppermute | solution.py:48
  60.1 1.2 copy-start.22
  62.2 0.9 copy-start.11
  62.2 1.1 copy-start.12
  62.4 0.8 copy-start.25
  62.4 0.8 copy-start.24
  62.4 0.8 copy-start.23
  62.4 0.8 copy-start.20
  63.4 11.5 %collective-permute-start.8 = (f32[2,48,576]{2,1,0:T(8,128)S(1)}, f32[2,48,576]{2,1,0:T(8,128)S(1)}, u32[]{:S(2)}, u32[]{:S(2)}) collective-permute-start(f32[2,48,576]{2,1,0:T(8,128)S(1)} %get-tuple-element.46), channel_id=1, source_target_pairs={{0,2},{2,4},{4,6},{6,8},{8,10},{10,12},{12,14},{1,3},{3,5},{5,7},{... | collective-permute-start | bytes 663560 | tf_op jit(solution)/shard_map/ppermute | solution.py:47
  65.4 14.8 %collective-permute-start.9 = (f32[2,48,576]{2,1,0:T(8,128)S(1)}, f32[2,48,576]{2,1,0:T(8,128)S(1)}, u32[]{:S(2)}, u32[]{:S(2)}) collective-permute-start(f32[2,48,576]{2,1,0:T(8,128)S(1)} %get-tuple-element.46), channel_id=1, source_target_pairs={{2,0},{4,2},{6,4},{8,6},{10,8},{12,10},{14,12},{3,1},{5,3},{7,5},{... | collective-permute-start | bytes 663560 | tf_op jit(solution)/shard_map/ppermute | solution.py:48
  80.8 6.0 %collective-permute-start.10 = (f32[6,2,576]{2,1,0:T(2,128)}, f32[6,2,576]{2,1,0:T(2,128)}, u32[]{:S(2)}, u32[]{:S(2)}) collective-permute-start(f32[6,2,576]{2,1,0:T(2,128)} %get-tuple-element.52), channel_id=1, source_target_pairs={{0,1},{2,3},{4,5},{6,7},{8,9},{10,11},{12,13},{14,15},{16,17},{18,... | collective-permute-start | bytes 82952 | tf_op jit(solution)/shard_map/ppermute | solution.py:47
  83.4 3.4 %collective-permute-start.11 = (f32[6,2,576]{2,1,0:T(2,128)}, f32[6,2,576]{2,1,0:T(2,128)}, u32[]{:S(2)}, u32[]{:S(2)}) collective-permute-start(f32[6,2,576]{2,1,0:T(2,128)} %get-tuple-element.53), channel_id=1, source_target_pairs={{1,0},{3,2},{5,4},{7,6},{9,8},{11,10},{13,12},{15,14},{17,16},{19,... | collective-permute-start | bytes 82952 | tf_op jit(solution)/shard_map/ppermute | solution.py:48
  88.3 0.9 copy-start.10
  89.5 11.0 %collective-permute-start.12 = (f32[2,48,576]{2,1,0:T(8,128)S(1)}, f32[2,48,576]{2,1,0:T(8,128)S(1)}, u32[]{:S(2)}, u32[]{:S(2)}) collective-permute-start(f32[2,48,576]{2,1,0:T(8,128)S(1)} %get-tuple-element.44), channel_id=1, source_target_pairs={{0,2},{2,4},{4,6},{6,8},{8,10},{10,12},{12,14},{1,3},{3,5},{5,7},{... | collective-permute-start | bytes 663560 | tf_op jit(solution)/shard_map/ppermute | solution.py:47
  91.4 14.9 %collective-permute-start.13 = (f32[2,48,576]{2,1,0:T(8,128)S(1)}, f32[2,48,576]{2,1,0:T(8,128)S(1)}, u32[]{:S(2)}, u32[]{:S(2)}) collective-permute-start(f32[2,48,576]{2,1,0:T(8,128)S(1)} %get-tuple-element.44), channel_id=1, source_target_pairs={{2,0},{4,2},{6,4},{8,6},{10,8},{12,10},{14,12},{3,1},{5,3},{7,5},{... | collective-permute-start | bytes 663560 | tf_op jit(solution)/shard_map/ppermute | solution.py:48
  107.0 4.9 %collective-permute-start.14 = (f32[6,2,576]{2,1,0:T(2,128)}, f32[6,2,576]{2,1,0:T(2,128)S(1)}, u32[]{:S(2)}, u32[]{:S(2)}) collective-permute-start(f32[6,2,576]{2,1,0:T(2,128)} %get-tuple-element.50), channel_id=1, source_target_pairs={{0,1},{2,3},{4,5},{6,7},{8,9},{10,11},{12,13},{14,15},{16,17},{18,... | collective-permute-start | bytes 82952 | tf_op jit(solution)/shard_map/ppermute | solution.py:47
  109.0 3.2 %copy-start.8 = (f32[2,48,576]{2,1,0:T(8,128)S(1)}, f32[2,48,576]{2,1,0:T(8,128)}, u32[]{:S(2)}) copy-start(f32[2,48,576]{2,1,0:T(8,128)} %copy-done.7) | copy-start | bytes 663556
  109.0 3.2 %collective-permute-start.15 = (f32[6,2,576]{2,1,0:T(2,128)S(1)}, f32[6,2,576]{2,1,0:T(2,128)S(1)}, u32[]{:S(2)}, u32[]{:S(2)}) collective-permute-start(f32[6,2,576]{2,1,0:T(2,128)S(1)} %get-tuple-element.51), channel_id=1, source_target_pairs={{1,0},{3,2},{5,4},{7,6},{9,8},{11,10},{13,12},{15,14},{17,16},{19,... | collective-permute-start | bytes 82952 | tf_op jit(solution)/shard_map/ppermute | solution.py:48
  113.0 1.0 copy-start.4
  113.1 1.4 copy-start.3
  114.6 14.4 %copy-start.14 = (f32[40,20]{0,1:T(8,128)S(1)}, f32[40,20]{0,1:T(8,128)}, u32[]{:S(2)}) copy-start(f32[40,20]{0,1:T(8,128)} %param.23) | copy-start | bytes 9604
  123.8 22.7 %copy-start.15 = (f32[2,48,20]{1,0,2:T(2,128)}, f32[2,48,20]{1,0,2:T(2,128)S(1)}, u32[]{:S(2)}) copy-start(f32[2,48,20]{1,0,2:T(2,128)S(1)} %reshape.214) | copy-start | bytes 23044
  124.0 22.5 %copy-start.16 = (f32[2,48,20]{1,0,2:T(2,128)}, f32[2,48,20]{1,0,2:T(2,128)S(1)}, u32[]{:S(2)}) copy-start(f32[2,48,20]{1,0,2:T(2,128)S(1)} %reshape.215) | copy-start | bytes 23044
  128.5 3.8 %collective-permute-start.20 = (f32[1,2,48,20]{2,3,1,0:T(8,128)S(1)}, f32[1,2,48,20]{2,3,1,0:T(8,128)S(1)}, u32[]{:S(2)}, u32[]{:S(2)}) collective-permute-start(f32[1,2,48,20]{2,3,1,0:T(8,128)S(1)} %bitcast.82), channel_id=1, source_target_pairs={{0,16},{16,0},{1,17},{17,1},{2,18},{18,2},{3,19},{19,3},{4,20},{20... | collective-permute-start | bytes 23048 | tf_op jit(solution)/shard_map/ppermute | solution.py:29
  132.5 5.9 %collective-permute-start.21 = (f32[1,48,40]{1,2,0:T(8,128)S(1)}, f32[1,48,40]{1,2,0:T(8,128)S(1)}, u32[]{:S(2)}, u32[]{:S(2)}) collective-permute-start(f32[1,48,40]{1,2,0:T(8,128)S(1)} %get-tuple-element.81), channel_id=1, source_target_pairs={{2,0},{4,2},{6,4},{8,6},{10,8},{12,10},{14,12},{3,1},{5,3},{7,5},{... | collective-permute-start | bytes 23048 | tf_op jit(solution)/shard_map/ppermute | solution.py:48
  134.5 6.6 %collective-permute-start.22 = (f32[1,48,40]{1,2,0:T(8,128)S(1)}, f32[1,48,40]{1,2,0:T(8,128)S(1)}, u32[]{:S(2)}, u32[]{:S(2)}) collective-permute-start(f32[1,48,40]{1,2,0:T(8,128)S(1)} %get-tuple-element.80), channel_id=1, source_target_pairs={{0,2},{2,4},{4,6},{6,8},{8,10},{10,12},{12,14},{1,3},{3,5},{5,7},{... | collective-permute-start | bytes 23048 | tf_op jit(solution)/shard_map/ppermute | solution.py:47
  141.1 4.3 %collective-permute-start.23 = (f32[4,1,40]{1,2,0:T(8,128)S(1)}, f32[4,1,40]{1,2,0:T(8,128)S(1)}, u32[]{:S(2)}, u32[]{:S(2)}) collective-permute-start(f32[4,1,40]{1,2,0:T(8,128)S(1)} %get-tuple-element.72), channel_id=1, source_target_pairs={{1,0},{3,2},{5,4},{7,6},{9,8},{11,10},{13,12},{15,14},{17,16},{19,... | collective-permute-start | bytes 1928 | tf_op jit(solution)/shard_map/ppermute | solution.py:48
  142.4 3.9 %collective-permute-start.24 = (f32[4,1,40]{1,2,0:T(8,128)S(1)}, f32[4,1,40]{1,2,0:T(8,128)S(1)}, u32[]{:S(2)}, u32[]{:S(2)}) collective-permute-start(f32[4,1,40]{1,2,0:T(8,128)S(1)} %get-tuple-element.73), channel_id=1, source_target_pairs={{0,1},{2,3},{4,5},{6,7},{8,9},{10,11},{12,13},{14,15},{16,17},{18,... | collective-permute-start | bytes 1928 | tf_op jit(solution)/shard_map/ppermute | solution.py:47
  146.5 5.9 %collective-permute-start.25 = (f32[1,2,48,20]{2,3,1,0:T(8,128)S(1)}, f32[1,2,48,20]{2,3,1,0:T(8,128)S(1)}, u32[]{:S(2)}, u32[]{:S(2)}) collective-permute-start(f32[1,2,48,20]{2,3,1,0:T(8,128)S(1)} %bitcast.81), channel_id=1, source_target_pairs={{0,16},{16,0},{1,17},{17,1},{2,18},{18,2},{3,19},{19,3},{4,20},{20... | collective-permute-start | bytes 23048 | tf_op jit(solution)/shard_map/ppermute | solution.py:29
  (9 other events, 6.3 us)
